TPU v7x, 32 devices: a whole 2x2x4 slice. The times are simulated.
32 devices in a mesh: groups: 2 (over x), tile: 16 (over z, y, core).
Axes of the slice: x: 2, y: 2, z: 4, core: 2. Of those that a mesh axis runs over, the one named last changes fastest.
Arguments:
- latent_rows: bfloat16 [4096, 256], P(('groups', 'tile')), parts along dimension 0, may hold values from -6 to 6
- line_order: int32 [128], P('groups'), parts along dimension 0, may hold values from 0 to 63, each once
- conv_weight: bfloat16 [3, 3, 3, 256, 128], replicated, may hold values from -0.078125 to 0.078125
- conv_bias: float32 [128], replicated, may hold values from -3 to 3
- blend_table: float32 [4, 8], replicated, may hold values from 0.25 to 4
- blend_ids: int32 [32], P('groups'), parts along dimension 0, may hold values from 0 to 3
Outputs:
- frames: bfloat16 [16, 32, 64, 128], P('groups', None, 'tile'), parts along dimension 0
There are 2 independent parts, one for each index of `groups`. A program takes and returns all parts, laid end to end along the dimension named above; an argument that names none is the same for every part. Nothing has to cross between parts.
Inputs may be any that keep to these rules, and one draw needn't show every extreme that they name: line_order is a permutation of the 64 latent lines.
All inputs are finite; a program needn't handle non-finite values.
Results may differ from a plain program's by a relative error of at most 0.001.
Values may be sent and summed in bfloat16 or wider, within the bound.
A program may use at most 64 MiB of HBM per device.

v0:
```python
import jax
import jax.numpy as jnp
from jax import lax
from jax.sharding import PartitionSpec as P

LT = 4
WD = 2


def from_behind(value, axis, steps):
    count = lax.axis_size(axis)
    initial, last = (max(0, -steps), min(count, count - steps))
    return lax.ppermute(value, axis, [(source, source + steps) for source in range(initial, last)])


def upsample(values):
    values = jnp.repeat(values, 2, axis=0)
    values = jnp.repeat(values, 2, axis=1)
    return jnp.repeat(values, 2, axis=2)


def decode_tile(window, conv_weight, conv_bias):
    upsampled = upsample(window)
    upsampled = jnp.concatenate([upsampled[:1], upsampled[:1], upsampled], axis=0)
    output = lax.conv_general_dilated(
        upsampled[None],
        conv_weight,
        (1, 1, 1),
        [(0, 0), (1, 1), (1, 1)],
        dimension_numbers=("NDHWC", "DHWIO", "NDHWC"),
        preferred_element_type=jnp.float32,
    )[0]
    return jax.nn.silu(output + conv_bias)


def blend_profile(blend_table, blend_ids, tile_at):
    kind_index = lax.dynamic_index_in_dim(blend_ids, tile_at, 0, keepdims=False)
    selector = (jnp.arange(blend_table.shape[0], dtype=jnp.int32) == kind_index).astype(jnp.float32)
    return jnp.sum(selector[:, None] * blend_table, axis=0)


def per_device(latent_rows, line_order, conv_weight, conv_bias, blend_table, blend_ids):
    tile_count = lax.axis_size("tile")
    position = lax.axis_index("tile")
    channels = latent_rows.shape[1]
    lines_dev = latent_rows.shape[0] // (WD * tile_count)
    blocks = latent_rows.reshape(lines_dev, tile_count, WD, channels)
    zero_col = jnp.zeros((lines_dev, 1, 1, channels), latent_rows.dtype)
    lower_cols = jnp.concatenate([zero_col, blocks[:, :-1, -1:]], axis=1)
    upper_cols = jnp.concatenate([blocks[:, 1:, :1], zero_col], axis=1)
    widened = jnp.concatenate([lower_cols, blocks, upper_cols], axis=2)
    received = lax.all_to_all(widened, "tile", split_axis=1, concat_axis=0, tiled=True)
    width_now = WD + 2
    line_count = received.shape[0]
    gathered_rows = received.reshape(line_count, width_now, channels)
    inverse = (
        jnp.zeros((line_count,), jnp.int32)
        .at[line_order]
        .set(jnp.arange(line_count, dtype=jnp.int32))
    )
    latent = gathered_rows[inverse].reshape(LT, line_count // LT, width_now, channels)
    decoded = decode_tile(latent, conv_weight, conv_bias)
    lower_at = jnp.maximum(position - 1, 0)
    upper_at = jnp.minimum(position + 1, tile_count - 1)
    has_lower = (position > 0).astype(jnp.float32)
    has_upper = (position < tile_count - 1).astype(jnp.float32)
    weight_self = blend_profile(blend_table, blend_ids, position)
    weight_lower = blend_profile(blend_table, blend_ids, lower_at)
    weight_upper = blend_profile(blend_table, blend_ids, upper_at)
    weighted = decoded * weight_self[None, None, :, None]
    from_lower = from_behind(weighted[:, :, -2:], "tile", 1)
    from_upper = from_behind(weighted[:, :, :2], "tile", -1)
    blended = weighted[:, :, 2:-2]
    blended = blended.at[:, :, :2].add(from_lower)
    blended = blended.at[:, :, -2:].add(from_upper)
    weight_sum = weight_self[2:-2]
    weight_sum = weight_sum.at[:2].add(has_lower * weight_lower[-2:])
    weight_sum = weight_sum.at[-2:].add(has_upper * weight_upper[:2])
    return (blended / weight_sum[None, None, :, None]).astype(jnp.bfloat16)


def solution(mesh):
    return jax.shard_map(
        per_device,
        mesh=mesh,
        in_specs=(P(("groups", "tile"), None), P("groups"), P(), P(), P(), P("groups")),
        out_specs=P("groups", None, "tile", None),
        check_vma=False,
    )
```

profile of v0, /device:TPU:5, one launch (start us, length us, event | category | flops | bytes accessed | tf_op | source)
XLA Modules:
  0.0 53.6 jit_solution(13139769069828558887)
XLA Ops:
  0.0 1.0 %reshape.160 = bf16[4,16,2,256]{3,2,1,0:T(2,128)(2,1)S(1)} reshape(bf16[128,256]{1,0:T(8,128)(2,1)} %param.14) | data formatting | bytes 131072 | tf_op jit(solution)/shard_map/reshape | solution.py:47
  1.0 0.1 fusion.11
  1.1 0.9 %fusion.6 = bf16[4,16,4,256]{3,2,0,1:T(4,128)(2,1)} fusion(bf16[4,15,1,256]{3,2,0,1:T(2,128)(2,1)S(1)} %get-tuple-element.59, bf16[4,15,1,256]{3,2,0,1:T(2,128)(2,1)S(1)} %get-tuple-element.58, bf16[4,16,2,256]{3,2,1,0:T(2,128)(2,1)S(1)} %reshape.160), kind=kLoop, calls=%fused_computation.15 | loop fusion | flops 655360 | bytes 258048 | tf_op jit(solution)/shard_map/concatenate | solution.py:51
  2.0 6.6 %all-to-all-start = ((bf16[4,16,4,256]{3,2,0,1:T(4,128)(2,1)}), bf16[4,16,4,256]{3,2,0,1:T(4,128)(2,1)S(1)}, u32[]{:S(2)}, u32[]{:S(2)}) async-start(bf16[4,16,4,256]{3,2,0,1:T(4,128)(2,1)} %fusion.6), calls=%async_computation | async-start | bytes 262144 | tf_op jit(solution)/shard_map/all_to_all | solution.py:52
  8.6 1.4 %fusion.12 = (s32[1]{0:T(128)}, s32[1]{0:T(128)}, s32[1]{0:T(128)}) fusion(s32[16]{0:T(128)} %param.19, s32[]{:T(128)S(6)} %max.3, s32[]{:T(128)S(6)} %select_n.16, s32[]{:T(128)S(6)} %select_n.17), kind=kLoop, calls=%fused_computation.33 | loop fusion | bytes 36 | tf_op jit(solution)/shard_map/jit(dynamic_index_in_dim)/dynamic_slice | solution.py:37
  10.1 0.6 %compare_convert_fusion.2 = f32[4]{0:T(128)S(1)} fusion(s32[]{:T(128)} %bitcast.10), kind=kLoop, calls=%fused_computation.26 | loop fusion | flops 8 | bytes 20 | tf_op jit(solution)/shard_map/convert_element_type | solution.py:38
  10.7 1.2 %compare_convert_fusion = (f32[4]{0:T(128)S(1)}, f32[4]{0:T(128)S(1)}) fusion(s32[]{:T(128)} %bitcast.12, s32[]{:T(128)} %bitcast.11), kind=kLoop, calls=%fused_computation.24 | loop fusion | flops 16 | bytes 40 | tf_op jit(solution)/shard_map/convert_element_type | solution.py:38
  11.9 0.8 %multiply_reduce_fusion = (f32[8]{0:T(128)S(1)}, f32[8]{0:T(128)S(1)}, f32[8]{0:T(128)S(1)}) fusion(f32[4,8]{1,0:T(4,128)} %param.18, f32[4]{0:T(128)S(1)} %get-tuple-element.63, f32[4]{0:T(128)S(1)} %compare_convert_fusion.2, f32[4]{0:T(128)S(1)} %get-tuple-element.64), kind=kLoop, calls=%fused_computation.21 | loop fusion | flops 168 | bytes 272 | tf_op jit(solution)/shard_map/reduce_sum | solution.py:39
  12.7 0.1 slice.131
  12.8 0.7 %compare_select_fusion.1 = s32[64]{0:T(128)S(1)} fusion(s32[64]{0:T(128)} %param.15), kind=kLoop, calls=%fused_computation.20 | loop fusion | flops 192 | bytes 512 | tf_op jit(solution)/shard_map/select_n | solution.py:59
  13.4 0.8 %scatter_custom_fusion = s32[64]{0:T(128)S(1)} fusion(s32[64]{0:T(128)S(1)} %compare_select_fusion.1, s32[64]{0:T(128)S(1)} %iota.18, s32[]{:T(128)} %constant.121.clone.1), kind=kCustom, calls=%fused_computation.29 | custom fusion | bytes 260 | tf_op jit(solution)/shard_map/scatter | solution.py:59
  14.2 0.3 all-to-all-done
  14.5 0.7 %gather_fusion = bf16[64,4,256]{2,1,0:T(4,128)(2,1)S(1)} fusion(bf16[64,4,256]{2,1,0:T(4,128)(2,1)S(1)} %bitcast.24, s32[1024]{0:T(1024)S(1)} %pad_clamp_fusion), kind=kCustom, calls=%fused_computation | custom fusion | bytes 262400 | tf_op jit(solution)/shard_map/gather | solution.py:61
  15.2 0.1 broadcast_in_dim.35
  15.4 0.1 broadcast_in_dim.38
  15.5 0.1 broadcast_in_dim.40
  15.7 1.7 %broadcast_in_dim.41 = bf16[8,32,4,2,256]{4,3,2,1,0:T(2,128)(2,1)} broadcast(bf16[8,32,4,256]{3,2,1,0:T(4,128)(2,1)S(1)} %bitcast.19), dimensions={0,1,2,4} | broadcast | bytes 1572864 | tf_op jit(solution)/shard_map/broadcast_in_dim | solution.py:19
  17.4 1.5 %reshape.165 = bf16[8,32,8,256]{3,2,1,0:T(8,128)(2,1)S(1)} reshape(bf16[8,32,4,2,256]{4,3,2,1,0:T(2,128)(2,1)} %broadcast_in_dim.41) | data formatting | bytes 2097152 | tf_op jit(solution)/shard_map/reshape | solution.py:19
  18.8 0.1 maximum_bitcast_fusion
  19.0 20.3 %fusion = f32[1,8,32,8,128]{4,0,3,2,1:T(1,128)S(1)} fusion(bf16[3,3,3,256,128]{4,3,2,1,0:T(8,128)(2,1)S(1)} %copy-done, bf16[1,10,32,8,256]{4,3,2,1,0:T(8,128)(2,1)S(1)} %maximum_bitcast_fusion), kind=kOutput, calls=%fused_computation.2 | convolution fusion | flops 3252682752 | bytes 4128768 | tf_op jit(solution)/shard_map/conv_general_dilated | solution.py:25
  39.3 0.3 multiply_multiply_fusion
  39.6 0.9 %fusion.10 = (f32[8,32,2,128]{3,2,1,0:T(2,128)S(1)}, f32[8,32,2,128]{3,2,1,0:T(2,128)}) fusion(f32[8,32,8,128]{3,2,1,0:T(8,128)S(1)} %multiply_multiply_fusion), kind=kLoop, calls=%fused_computation.31 | loop fusion | bytes 1048576 | tf_op jit(solution)/shard_map/slice | solution.py:72
  40.5 3.1 %collective-permute-start = (f32[8,32,2,128]{3,2,1,0:T(2,128)}, f32[8,32,2,128]{3,2,1,0:T(2,128)S(1)}, u32[]{:S(2)}, u32[]{:S(2)}) collective-permute-start(f32[8,32,2,128]{3,2,1,0:T(2,128)} %get-tuple-element.57), channel_id=1, source_target_pairs={{0,1},{1,2},{2,3},{3,4},{4,5},{5,6},{6,7},{7,8},{8,9},{9,10},{10,1... | collective-permute-start | bytes 786440 | tf_op jit(solution)/shard_map/ppermute | solution.py:13
  43.5 0.1 constant_dynamic-update-slice_fusion.1
  43.6 0.2 constant_dynamic-update-slice_fusion
  43.8 0.1 slice.141
  43.9 1.9 %collective-permute-start.1 = (f32[8,32,2,128]{3,2,1,0:T(2,128)S(1)}, f32[8,32,2,128]{3,2,1,0:T(2,128)S(1)}, u32[]{:S(2)}, u32[]{:S(2)}) collective-permute-start(f32[8,32,2,128]{3,2,1,0:T(2,128)S(1)} %get-tuple-element.56), channel_id=1, source_target_pairs={{1,0},{2,1},{3,2},{4,3},{5,4},{6,5},{7,6},{8,7},{9,8},{10,9},{11,1... | collective-permute-start | bytes 786440 | tf_op jit(solution)/shard_map/ppermute | solution.py:13
  45.8 1.3 %collective-permute-done = f32[8,32,2,128]{3,2,1,0:T(2,128)S(1)} collective-permute-done((f32[8,32,2,128]{3,2,1,0:T(2,128)}, f32[8,32,2,128]{3,2,1,0:T(2,128)S(1)}, u32[]{:S(2)}, u32[]{:S(2)}) %collective-permute-start) | collective-permute-done | bytes 262176 | tf_op jit(solution)/shard_map/ppermute | solution.py:13
  47.1 0.2 fusion.3
  47.4 5.1 %collective-permute-done.1 = f32[8,32,2,128]{3,2,1,0:T(2,128)S(1)} collective-permute-done((f32[8,32,2,128]{3,2,1,0:T(2,128)S(1)}, f32[8,32,2,128]{3,2,1,0:T(2,128)S(1)}, u32[]{:S(2)}, u32[]{:S(2)}) %collective-permute-start.1) | collective-permute-done | bytes 262176 | tf_op jit(solution)/shard_map/ppermute | solution.py:13
  52.5 0.3 fusion.2
  52.8 0.9 %divide_convert_fusion = bf16[8,32,4,128]{3,2,1,0:T(4,128)(2,1)} fusion(f32[8,32,4,128]{3,2,1,0:T(4,128)S(1)} %fusion.2, f32[4]{0:T(128)S(1)} %constant_dynamic-update-slice_fusion), kind=kLoop, calls=%fused_computation.6 | loop fusion | flops 262144 | bytes 786448 | tf_op jit(solution)/shard_map/convert_element_type | solution.py:79
  (10 shorter events, 0.1 us)
Async XLA Ops:
  0.0 18.9 %copy-start = (bf16[3,3,3,256,128]{4,3,2,1,0:T(8,128)(2,1)S(1)}, bf16[3,3,3,256,128]{4,3,2,1,0:T(8,128)(2,1)}, u32[]{:S(2)}) copy-start(bf16[3,3,3,256,128]{4,3,2,1,0:T(8,128)(2,1)} %param.16) | copy-start | bytes 5308420
  2.0 12.5 %all-to-all-start = ((bf16[4,16,4,256]{3,2,0,1:T(4,128)(2,1)}), bf16[4,16,4,256]{3,2,0,1:T(4,128)(2,1)S(1)}, u32[]{:S(2)}, u32[]{:S(2)}) async-start(bf16[4,16,4,256]{3,2,0,1:T(4,128)(2,1)} %fusion.6), calls=%async_computation | async-start | bytes 262144 | tf_op jit(solution)/shard_map/all_to_all | solution.py:52
  19.0 20.3 %copy-start.1 = (f32[128]{0:T(128)S(1)}, f32[128]{0:T(128)}, u32[]{:S(2)}) copy-start(f32[128]{0:T(128)} %param.17) | copy-start | bytes 1540
  40.5 6.7 %collective-permute-start = (f32[8,32,2,128]{3,2,1,0:T(2,128)}, f32[8,32,2,128]{3,2,1,0:T(2,128)S(1)}, u32[]{:S(2)}, u32[]{:S(2)}) collective-permute-start(f32[8,32,2,128]{3,2,1,0:T(2,128)} %get-tuple-element.57), channel_id=1, source_target_pairs={{0,1},{1,2},{2,3},{3,4},{4,5},{5,6},{6,7},{7,8},{8,9},{9,10},{10,1... | collective-permute-start | bytes 786440 | tf_op jit(solution)/shard_map/ppermute | solution.py:13
  43.9 8.6 %collective-permute-start.1 = (f32[8,32,2,128]{3,2,1,0:T(2,128)S(1)}, f32[8,32,2,128]{3,2,1,0:T(2,128)S(1)}, u32[]{:S(2)}, u32[]{:S(2)}) collective-permute-start(f32[8,32,2,128]{3,2,1,0:T(2,128)S(1)} %get-tuple-element.56), channel_id=1, source_target_pairs={{1,0},{2,1},{3,2},{4,3},{5,4},{6,5},{7,6},{8,7},{9,8},{10,9},{11,1... | collective-permute-start | bytes 786440 | tf_op jit(solution)/shard_map/ppermute | solution.py:13
where the time goes:
time: 54 us; the launch traced here: 53.6 us
  matrix products  20.3 us (38%)
  starting transfers between devices  11.6 us (21%)
  local copies, waits for them, and re-layouts  8.63 us (16%)
  waiting for transfers between devices  6.73 us (12%)
  other arithmetic  6.2 us (11%)
    conv_general_dilated x1, matrix products, decode_tile(): lax.conv_general_dilated(upsampled[None], conv_weight, (1, 1, 1), [(0, 0)...  20.3 us
    all_to_all x1, starting transfers between devices, per_device(): lax.all_to_all(widened, 'tile', split_axis=1, concat_axis=0, tiled=True)  6.63 us
    ppermute x2, waiting for transfers between devices, from_behind(): lax.ppermute(value, axis, [(source, source + steps) for source in range(i...  6.41 us
    ppermute x2, starting transfers between devices, from_behind(): lax.ppermute(value, axis, [(source, source + steps) for source in range(i...  4.97 us
    broadcast_in_dim x3, local copies, waits for them, and re-layouts, upsample(): return jnp.repeat(values, 2, axis=2)  1.84 us
    convert_element_type x2, other arithmetic, blend_profile(): (jnp.arange(blend_table.shape[0], dtype=jnp.int32) == kind_index).astype(...  1.83 us
    reshape x1, local copies, waits for them, and re-layouts, upsample(): return jnp.repeat(values, 2, axis=2)  1.47 us
    dynamic_slice x1, local copies, waits for them, and re-layouts, blend_profile(): kind_index = lax.dynamic_index_in_dim(blend_ids, tile_at, 0, keepdims=False)  1.42 us
  transfers between devices with their start and end apart: 3, of which 3 were waited for; matrix products, arithmetic and copies ran while one was open for 11% of the time, Pallas kernels for 0%

commit v1 on v0

--- a/solution.py
+++ b/solution.py
@@ -49,7 +49,10 @@
     lower_cols = jnp.concatenate([zero_col, blocks[:, :-1, -1:]], axis=1)
     upper_cols = jnp.concatenate([blocks[:, 1:, :1], zero_col], axis=1)
     widened = jnp.concatenate([lower_cols, blocks, upper_cols], axis=2)
-    received = lax.all_to_all(widened, "tile", split_axis=1, concat_axis=0, tiled=True)
+    received = jnp.concatenate(
+        lax.all_to_all(jnp.stack(jnp.split(widened, lax.axis_size("tile"), axis=1)), "tile", 0, 0),
+        axis=0,
+    )
     width_now = WD + 2
     line_count = received.shape[0]
     gathered_rows = received.reshape(line_count, width_now, channels)

time: 54 us -> 63 us (1.17)
  local copies, waits for them, and re-layouts: 8.63 us -> 18.3 us
  other arithmetic: 6.2 us -> 5.54 us
    unnamed x4 -> x19, local copies, waits for them, and re-layouts: 0.01 us -> 9.05 us
    concatenate x1, other arithmetic: 0.91 us -> 0.25 us  [per_device(): widened = jnp.concatenate([lower_cols, blocks, upper_cols], axis=2)]
  transfers between devices with their start and end apart: 3 -> 3, of which waited for: 3 -> 3; matrix products, arithmetic and copies ran while one was open for 11% -> 10% of each run, Pallas kernels for 0% -> 0%
where the time goes in v1:
time: 63 us; the launch traced here: 62.6 us
  matrix products  20.3 us (32%)
  local copies, waits for them, and re-layouts  18.3 us (29%)
  starting transfers between devices  11.6 us (18%)
  waiting for transfers between devices  6.73 us (11%)
  other arithmetic  5.54 us (9%)
    conv_general_dilated x1, matrix products, decode_tile(): lax.conv_general_dilated(upsampled[None], conv_weight, (1, 1, 1), [(0, 0)...  20.3 us
    unnamed x19, local copies, waits for them, and re-layouts  9.05 us
    all_to_all x1, starting transfers between devices, per_device(): lax.all_to_all(jnp.stack(jnp.split(widened, lax.axis_size('tile'), axis=1...  6.63 us
    ppermute x2, waiting for transfers between devices, from_behind(): lax.ppermute(value, axis, [(source, source + steps) for source in range(i...  6.41 us
    ppermute x2, starting transfers between devices, from_behind(): lax.ppermute(value, axis, [(source, source + steps) for source in range(i...  4.97 us
    broadcast_in_dim x3, local copies, waits for them, and re-layouts, upsample(): return jnp.repeat(values, 2, axis=2)  1.84 us
    convert_element_type x2, other arithmetic, blend_profile(): (jnp.arange(blend_table.shape[0], dtype=jnp.int32) == kind_index).astype(...  1.83 us
    reshape x1, local copies, waits for them, and re-layouts, upsample(): return jnp.repeat(values, 2, axis=2)  1.47 us
  transfers between devices with their start and end apart: 3, of which 3 were waited for; matrix products, arithmetic and copies ran while one was open for 10% of the time, Pallas kernels for 0%

profile of v1, /device:TPU:5, one launch (start us, length us, event | category | flops | bytes accessed | tf_op | source)
XLA Modules:
  0.0 62.6 jit_solution(13643712092157361878)
XLA Ops:
  0.0 1.0 %reshape.156 = bf16[4,16,2,256]{3,2,1,0:T(2,128)(2,1)S(1)} reshape(bf16[128,256]{1,0:T(8,128)(2,1)} %param.14) | data formatting | bytes 131072 | tf_op jit(solution)/shard_map/reshape | solution.py:47
  1.4 0.6 constant_dynamic-update-slice_fusion.15
  2.0 0.6 constant_dynamic-update-slice_fusion.14
  2.6 0.6 constant_dynamic-update-slice_fusion.13
  3.2 0.6 constant_dynamic-update-slice_fusion.12
  3.8 0.6 constant_dynamic-update-slice_fusion.11
  4.4 0.6 constant_dynamic-update-slice_fusion.10
  5.0 0.6 constant_dynamic-update-slice_fusion.9
  5.6 0.6 constant_dynamic-update-slice_fusion.8
  6.2 0.6 constant_dynamic-update-slice_fusion.7
  6.8 0.6 constant_dynamic-update-slice_fusion.6
  7.4 0.6 constant_dynamic-update-slice_fusion.5
  9.2 0.6 constant_dynamic-update-slice_fusion.2
  9.8 0.6 constant_dynamic-update-slice_fusion.1
  10.4 0.6 constant_dynamic-update-slice_fusion
  11.0 6.6 %all-to-all-start = ((bf16[16,4,1,4,256]{4,3,1,2,0:T(4,128)(2,1)}), bf16[16,4,1,4,256]{4,3,1,2,0:T(4,128)(2,1)S(1)}, u32[]{:S(2)}, u32[]{:S(2)}) async-start(bf16[16,4,1,4,256]{4,3,1,2,0:T(4,128)(2,1)} %constant_dynamic-update-slice_fusion), calls=%async_computation | async-start | bytes 262144 | tf_op jit(solution)/shard_map/all_to_all | solution.py:53
  17.6 1.4 %fusion.12 = (s32[1]{0:T(128)}, s32[1]{0:T(128)}, s32[1]{0:T(128)}) fusion(s32[16]{0:T(128)} %param.19, s32[]{:T(128)S(6)} %max.3, s32[]{:T(128)S(6)} %select_n.16, s32[]{:T(128)S(6)} %select_n.17), kind=kLoop, calls=%fused_computation.65 | loop fusion | bytes 36 | tf_op jit(solution)/shard_map/jit(dynamic_index_in_dim)/dynamic_slice | solution.py:37
  19.1 0.6 %compare_convert_fusion.2 = f32[4]{0:T(128)S(1)} fusion(s32[]{:T(128)} %bitcast.24), kind=kLoop, calls=%fused_computation.58 | loop fusion | flops 8 | bytes 20 | tf_op jit(solution)/shard_map/convert_element_type | solution.py:38
  19.7 1.2 %compare_convert_fusion = (f32[4]{0:T(128)S(1)}, f32[4]{0:T(128)S(1)}) fusion(s32[]{:T(128)} %bitcast.26, s32[]{:T(128)} %bitcast.25), kind=kLoop, calls=%fused_computation.56 | loop fusion | flops 16 | bytes 40 | tf_op jit(solution)/shard_map/convert_element_type | solution.py:38
  20.9 0.8 %multiply_reduce_fusion = (f32[8]{0:T(128)S(1)}, f32[8]{0:T(128)S(1)}, f32[8]{0:T(128)S(1)}) fusion(f32[4,8]{1,0:T(4,128)} %param.18, f32[4]{0:T(128)S(1)} %get-tuple-element.63, f32[4]{0:T(128)S(1)} %compare_convert_fusion.2, f32[4]{0:T(128)S(1)} %get-tuple-element.64), kind=kLoop, calls=%fused_computation.53 | loop fusion | flops 168 | bytes 272 | tf_op jit(solution)/shard_map/reduce_sum | solution.py:39
  21.8 0.7 %compare_select_fusion.1 = s32[64]{0:T(128)S(1)} fusion(s32[64]{0:T(128)} %param.15), kind=kLoop, calls=%fused_computation.52 | loop fusion | flops 192 | bytes 512 | tf_op jit(solution)/shard_map/select_n | solution.py:62
  22.4 0.8 %scatter_custom_fusion = s32[64]{0:T(128)S(1)} fusion(s32[64]{0:T(128)S(1)} %compare_select_fusion.1, s32[64]{0:T(128)S(1)} %iota.18, s32[]{:T(128)} %constant.121.clone.1), kind=kCustom, calls=%fused_computation.61 | custom fusion | bytes 260 | tf_op jit(solution)/shard_map/scatter | solution.py:62
  23.5 0.7 %gather_fusion = bf16[64,4,256]{2,1,0:T(4,128)(2,1)S(1)} fusion(bf16[64,4,256]{2,1,0:T(4,128)(2,1)S(1)} %bitcast.114, s32[1024]{0:T(1024)S(1)} %pad_clamp_fusion), kind=kCustom, calls=%fused_computation | custom fusion | bytes 262400 | tf_op jit(solution)/shard_map/gather | solution.py:64
  24.7 1.7 %broadcast_in_dim.41 = bf16[8,32,4,2,256]{4,3,2,1,0:T(2,128)(2,1)} broadcast(bf16[8,32,4,256]{3,2,1,0:T(4,128)(2,1)S(1)} %bitcast.109), dimensions={0,1,2,4} | broadcast | bytes 1572864 | tf_op jit(solution)/shard_map/broadcast_in_dim | solution.py:19
  26.4 1.5 %reshape.160 = bf16[8,32,8,256]{3,2,1,0:T(8,128)(2,1)S(1)} reshape(bf16[8,32,4,2,256]{4,3,2,1,0:T(2,128)(2,1)} %broadcast_in_dim.41) | data formatting | bytes 2097152 | tf_op jit(solution)/shard_map/reshape | solution.py:19
  28.0 20.3 %fusion = f32[1,8,32,8,128]{4,0,3,2,1:T(1,128)S(1)} fusion(bf16[3,3,3,256,128]{4,3,2,1,0:T(8,128)(2,1)S(1)} %copy-done, bf16[1,10,32,8,256]{4,3,2,1,0:T(8,128)(2,1)S(1)} %maximum_bitcast_fusion), kind=kOutput, calls=%fused_computation.2 | convolution fusion | flops 3252682752 | bytes 4128768 | tf_op jit(solution)/shard_map/conv_general_dilated | solution.py:25
  48.6 0.9 %fusion.10 = (f32[8,32,2,128]{3,2,1,0:T(2,128)S(1)}, f32[8,32,2,128]{3,2,1,0:T(2,128)}) fusion(f32[8,32,8,128]{3,2,1,0:T(8,128)S(1)} %multiply_multiply_fusion), kind=kLoop, calls=%fused_computation.63 | loop fusion | bytes 1048576 | tf_op jit(solution)/shard_map/slice | solution.py:75
  49.5 3.1 %collective-permute-start = (f32[8,32,2,128]{3,2,1,0:T(2,128)}, f32[8,32,2,128]{3,2,1,0:T(2,128)S(1)}, u32[]{:S(2)}, u32[]{:S(2)}) collective-permute-start(f32[8,32,2,128]{3,2,1,0:T(2,128)} %get-tuple-element.57), channel_id=1, source_target_pairs={{0,1},{1,2},{2,3},{3,4},{4,5},{5,6},{6,7},{7,8},{8,9},{9,10},{10,1... | collective-permute-start | bytes 786440 | tf_op jit(solution)/shard_map/ppermute | solution.py:13
  52.9 1.9 %collective-permute-start.1 = (f32[8,32,2,128]{3,2,1,0:T(2,128)S(1)}, f32[8,32,2,128]{3,2,1,0:T(2,128)S(1)}, u32[]{:S(2)}, u32[]{:S(2)}) collective-permute-start(f32[8,32,2,128]{3,2,1,0:T(2,128)S(1)} %get-tuple-element.56), channel_id=1, source_target_pairs={{1,0},{2,1},{3,2},{4,3},{5,4},{6,5},{7,6},{8,7},{9,8},{10,9},{11,1... | collective-permute-start | bytes 786440 | tf_op jit(solution)/shard_map/ppermute | solution.py:13
  54.8 1.3 %collective-permute-done = f32[8,32,2,128]{3,2,1,0:T(2,128)S(1)} collective-permute-done((f32[8,32,2,128]{3,2,1,0:T(2,128)}, f32[8,32,2,128]{3,2,1,0:T(2,128)S(1)}, u32[]{:S(2)}, u32[]{:S(2)}) %collective-permute-start) | collective-permute-done | bytes 262176 | tf_op jit(solution)/shard_map/ppermute | solution.py:13
  56.4 5.1 %collective-permute-done.1 = f32[8,32,2,128]{3,2,1,0:T(2,128)S(1)} collective-permute-done((f32[8,32,2,128]{3,2,1,0:T(2,128)S(1)}, f32[8,32,2,128]{3,2,1,0:T(2,128)S(1)}, u32[]{:S(2)}, u32[]{:S(2)}) %collective-permute-start.1) | collective-permute-done | bytes 262176 | tf_op jit(solution)/shard_map/ppermute | solution.py:13
  61.8 0.9 %divide_convert_fusion = bf16[8,32,4,128]{3,2,1,0:T(4,128)(2,1)} fusion(f32[8,32,4,128]{3,2,1,0:T(4,128)S(1)} %fusion.2, f32[4]{0:T(128)S(1)} %constant_dynamic-update-slice_fusion.16), kind=kLoop, calls=%fused_computation.6 | loop fusion | flops 262144 | bytes 786448 | tf_op jit(solution)/shard_map/convert_element_type | solution.py:82
  (26 shorter events, 3.6 us)
Async XLA Ops:
  0.0 27.9 %copy-start = (bf16[3,3,3,256,128]{4,3,2,1,0:T(8,128)(2,1)S(1)}, bf16[3,3,3,256,128]{4,3,2,1,0:T(8,128)(2,1)}, u32[]{:S(2)}) copy-start(bf16[3,3,3,256,128]{4,3,2,1,0:T(8,128)(2,1)} %param.16) | copy-start | bytes 5308420
  11.0 12.5 %all-to-all-start = ((bf16[16,4,1,4,256]{4,3,1,2,0:T(4,128)(2,1)}), bf16[16,4,1,4,256]{4,3,1,2,0:T(4,128)(2,1)S(1)}, u32[]{:S(2)}, u32[]{:S(2)}) async-start(bf16[16,4,1,4,256]{4,3,1,2,0:T(4,128)(2,1)} %constant_dynamic-update-slice_fusion), calls=%async_computation | async-start | bytes 262144 | tf_op jit(solution)/shard_map/all_to_all | solution.py:53
  28.0 20.3 %copy-start.1 = (f32[128]{0:T(128)S(1)}, f32[128]{0:T(128)}, u32[]{:S(2)}) copy-start(f32[128]{0:T(128)} %param.17) | copy-start | bytes 1540
  49.5 6.7 %collective-permute-start = (f32[8,32,2,128]{3,2,1,0:T(2,128)}, f32[8,32,2,128]{3,2,1,0:T(2,128)S(1)}, u32[]{:S(2)}, u32[]{:S(2)}) collective-permute-start(f32[8,32,2,128]{3,2,1,0:T(2,128)} %get-tuple-element.57), channel_id=1, source_target_pairs={{0,1},{1,2},{2,3},{3,4},{4,5},{5,6},{6,7},{7,8},{8,9},{9,10},{10,1... | collective-permute-start | bytes 786440 | tf_op jit(solution)/shard_map/ppermute | solution.py:13
  52.9 8.6 %collective-permute-start.1 = (f32[8,32,2,128]{3,2,1,0:T(2,128)S(1)}, f32[8,32,2,128]{3,2,1,0:T(2,128)S(1)}, u32[]{:S(2)}, u32[]{:S(2)}) collective-permute-start(f32[8,32,2,128]{3,2,1,0:T(2,128)S(1)} %get-tuple-element.56), channel_id=1, source_target_pairs={{1,0},{2,1},{3,2},{4,3},{5,4},{6,5},{7,6},{8,7},{9,8},{10,9},{11,1... | collective-permute-start | bytes 786440 | tf_op jit(solution)/shard_map/ppermute | solution.py:13
